TPU v7x, 128 devices: a whole 4x4x4 slice. The times are simulated.
128 devices in a mesh: stream: 64 (over z, y, x), seq: 2 (over core).
Axes of the slice: x: 4, y: 4, z: 4, core: 2. Of those that a mesh axis runs over, the one named last changes fastest.
Arguments:
- head_inputs: bfloat16 [64, 3072, 1536], P('stream', 'seq'), may hold values from -6 to 6
- state_maps: bfloat16 [64, 3072, 256], P('stream', 'seq'), may hold values from -2.1 to 2.1
- step_logits: float32 [64, 24, 3072], P('stream', None, 'seq'), may hold values from -3 to 5.5
- log_rates: float32 [24], replicated, may hold values from -7 to 0
- step_bias: float32 [24], replicated, may hold values from -6 to -2
- skip_gain: float32 [24], replicated, may hold values from 0.25 to 1.75
- old_states: float32 [64, 24, 64, 128], P('stream', 'seq'), may hold values from -6 to 6
- old_owner: int32 [64], replicated, may hold values from 0 to 63, as said below
- doc_starts: int32 [64, 2], P('stream'), may hold values from 0 to 3071
- grad_output: bfloat16 [64, 3072, 1536], P('stream', 'seq'), may hold values from -6 to 6
Outputs:
- layer_out: bfloat16 [64, 3072, 1536], P('stream', 'seq')
- grad_inputs: bfloat16 [64, 3072, 1536], P('stream', 'seq')
- grad_maps: bfloat16 [64, 3072, 256], P('stream', 'seq')
- grad_logits: float32 [64, 24, 3072], P('stream', None, 'seq')
- grad_rates: float32 [24], replicated
- grad_bias: float32 [24], replicated
- grad_skip: float32 [24], replicated
Inputs may be any that keep to these rules, and one draw needn't show every extreme that they name: A permutation of the 64 stream indices: new stream s continues old stream old_owner[s]. `doc_starts`: positions in a stream's segment where a document starts and the state is cleared; entries may repeat.
All inputs are finite; a program needn't handle non-finite values.
Results may differ from a plain program's by a relative error of at most 0.013.
Values sent between devices are 32-bit elements; how exact they have to be, the bound alone decides.
No kernel may reach another device: no remote copies, remote signals or barrier semaphores. Data moves between devices by JAX's collectives and lax.ppermute only.
A program may use at most 192 MiB of HBM per device.

v0:
```python
import jax
import jax.numpy as jnp
from jax import lax
from jax.sharding import PartitionSpec as P

GROUP = 256


def shifted_2(shard, axis, by):
    size = lax.axis_size(axis)
    pairs = [(i, i + by) for i in range(size) if 0 <= i + by < size]
    return lax.ppermute(shard, axis, pairs)


def decay_terms(logits_part, flags_part, log_rates, step_bias):
    step_size = jax.nn.softplus(logits_part + step_bias[:, None])
    cum_decay = jnp.cumsum(-step_size * jnp.exp(log_rates)[:, None], axis=-1)
    doc_index = jnp.cumsum(flags_part, axis=-1)
    return (step_size, cum_decay, doc_index)


def group_states(inputs_c, maps_c, logits_c, flags_c, log_rates, step_bias):
    step_size, cum_decay, doc_index = decay_terms(logits_c, flags_c, log_rates, step_bias)
    state_n = maps_c.shape[-1] // 2
    b_part = maps_c[:, :, :state_n].astype(jnp.float32)
    same_doc = doc_index == doc_index[:, -1:]
    weight = (
        jnp.where(same_doc[:, None, :], jnp.exp(cum_decay[:, :, -1:] - cum_decay), 0.0) * step_size
    )
    b_weighted = (weight[:, :, :, None] * b_part[:, None, :, :]).astype(jnp.bfloat16)
    states = jnp.einsum("cjhp,chjn->chpn", inputs_c, b_weighted, preferred_element_type=jnp.float32)
    decays = jnp.where(doc_index[:, -1:] == 0, jnp.exp(cum_decay[:, :, -1]), 0.0)
    return (states, decays)


def group_inputs(start_state, states, decays):

    def advance(carry, members):
        group_state, group_decay = members
        return (group_decay[:, None, None] * carry + group_state, carry)

    return lax.scan(advance, start_state, (states, decays))


def one_group(inputs_q, maps_q, logits_q, flags_q, starts_q, log_rates, step_bias, skip_gain):
    step_size, cum_decay, doc_index = decay_terms(logits_q, flags_q, log_rates, step_bias)
    state_n = maps_q.shape[-1] // 2
    b_part = maps_q[:, :state_n]
    c_part = maps_q[:, state_n:]
    scores = jnp.dot(c_part, b_part.T, preferred_element_type=jnp.float32)
    position = jnp.arange(maps_q.shape[0])
    visible = (position[None, :] <= position[:, None]) & (doc_index[None, :] == doc_index[:, None])
    log_gaps = jnp.where(visible[None], cum_decay[:, :, None] - cum_decay[:, None, :], -jnp.inf)
    mixing = (scores[None] * jnp.exp(log_gaps) * step_size[:, None, :]).astype(jnp.bfloat16)
    local_part = jnp.einsum("hij,jhp->ihp", mixing, inputs_q, preferred_element_type=jnp.float32)
    inflow = jnp.where(doc_index[None, :] == 0, jnp.exp(cum_decay), 0.0)
    carried = jnp.einsum(
        "in,hpn->ihp", c_part.astype(jnp.float32), starts_q, precision=lax.Precision.HIGHEST
    )
    summed = (
        local_part
        + carried * inflow.T[:, :, None]
        + skip_gain[None, :, None] * inputs_q.astype(jnp.float32)
    )
    return summed.reshape(inputs_q.shape[0], -1).astype(jnp.bfloat16)


def outputs(inputs_c, maps_c, logits_c, flags_c, log_rates, step_bias, skip_gain, starts_c):

    def per_group(carry, members):
        inputs_q, maps_q, logits_q, flags_q, starts_q = members
        return (
            carry,
            jax.checkpoint(one_group)(
                inputs_q, maps_q, logits_q, flags_q, starts_q, log_rates, step_bias, skip_gain
            ),
        )

    _, result = lax.scan(per_group, 0, (inputs_c, maps_c, logits_c, flags_c, starts_c))
    return result


def shards(
    head_inputs,
    state_maps,
    step_logits,
    log_rates,
    step_bias,
    skip_gain,
    old_states,
    old_owner,
    doc_starts,
    grad_output,
):
    length = head_inputs.shape[1]
    head_count = step_logits.shape[1]
    head_dim = old_states.shape[2]
    state_n = old_states.shape[3]
    groups = length // GROUP
    seq_index = lax.axis_index("seq")
    stream_index = lax.axis_index("stream")
    position = seq_index * length + lax.iota(jnp.int32, length)
    reset_flags = jnp.any(doc_starts[0][:, None] == position[None, :], axis=0).astype(jnp.int32)
    gathered = lax.all_gather(old_states, "stream", axis=0, tiled=True)
    own_block = lax.dynamic_index_in_dim(gathered, old_owner[stream_index], 0, keepdims=False)
    start_state = lax.all_gather(own_block, "seq", axis=0, tiled=True)
    inputs_c = head_inputs[0].reshape(groups, GROUP, head_count, head_dim)
    maps_c = state_maps[0].reshape(groups, GROUP, 2 * state_n)
    logits_c = step_logits[0].reshape(head_count, groups, GROUP).transpose(1, 0, 2)
    flags_c = reset_flags.reshape(groups, GROUP)

    def state_part(inputs_c, maps_c, logits_c, log_rates, step_bias):
        return group_states(inputs_c, maps_c, logits_c, flags_c, log_rates, step_bias)

    (states, decays), pull_states = jax.vjp(
        state_part, inputs_c, maps_c, logits_c, log_rates, step_bias
    )
    empty_state = jnp.zeros((head_count, head_dim, state_n), jnp.float32)
    local_state, _ = group_inputs(empty_state, states, decays)
    shard_decay = jnp.prod(decays, axis=0)
    is_first = seq_index == 0

    def forward_turn(counter, entering):
        leaving = shard_decay[:, None, None] * entering + local_state
        shifted = shifted_2(leaving, "seq", 1)
        return jnp.where(is_first, start_state, shifted)

    entry_state = lax.fori_loop(0, lax.axis_size("seq") - 1, forward_turn, start_state)
    (exit_state, starts_c), pull_inputs = jax.vjp(group_inputs, entry_state, states, decays)

    def output_part(inputs_c, maps_c, logits_c, log_rates, step_bias, skip_gain, starts_c):
        return outputs(
            inputs_c, maps_c, logits_c, flags_c, log_rates, step_bias, skip_gain, starts_c
        )

    result, pull_output = jax.vjp(
        output_part, inputs_c, maps_c, logits_c, log_rates, step_bias, skip_gain, starts_c
    )
    grads_c = grad_output[0].reshape(groups, GROUP, head_count * head_dim)
    in_first, maps_first, logits_first, rates_first, bias_first, skip_total, grad_starts = (
        pull_output(grads_c)
    )
    from_output = pull_inputs((jnp.zeros_like(exit_state), grad_starts))[0]

    def backward_turn(counter, leaving_grad):
        entering_grad = shard_decay[:, None, None] * leaving_grad + from_output
        return shifted_2(entering_grad, "seq", -1)

    exit_grad = lax.fori_loop(0, lax.axis_size("seq") - 1, backward_turn, empty_state)
    _, grad_states, grad_decays = pull_inputs((exit_grad, grad_starts))
    in_second, maps_second, logits_second, rates_second, bias_second = pull_states(
        (grad_states, grad_decays)
    )
    rates_total, bias_total, skip_sum = lax.psum(
        (rates_first + rates_second, bias_first + bias_second, skip_total), ("stream", "seq")
    )
    grad_logits = (logits_first + logits_second).transpose(1, 0, 2).reshape(1, head_count, length)
    return (
        result.reshape(1, length, -1),
        (in_first + in_second).reshape(1, length, -1),
        (maps_first + maps_second).reshape(1, length, -1),
        grad_logits,
        rates_total,
        bias_total,
        skip_sum,
    )


def solution(mesh):
    return jax.shard_map(
        shards,
        mesh=mesh,
        in_specs=(
            P("stream", "seq", None),
            P("stream", "seq", None),
            P("stream", None, "seq"),
            P(),
            P(),
            P(),
            P("stream", "seq", None, None),
            P(),
            P("stream", None),
            P("stream", "seq", None),
        ),
        out_specs=(
            P("stream", "seq", None),
            P("stream", "seq", None),
            P("stream", "seq", None),
            P("stream", None, "seq"),
            P(),
            P(),
            P(),
        ),
        check_vma=False,
    )
```

profile of v0, /device:TPU:1, one launch (start us, length us, event | category | flops | bytes accessed | tf_op | source)
XLA Modules:
  0.0 601.4 jit_solution(6530939128043399756)
XLA Ops:
  21.2 12.9 %reshape.634 = bf16[6,256,24,64]{3,2,1,0:T(8,128)(2,1)} reshape(bf16[1,1536,1536]{2,1,0:T(8,128)(2,1)} %param.22) | data formatting | bytes 9437184 | tf_op jit(solution)/shard_map/reshape;squeeze | solution.py:107
  34.1 10.3 %copy.231 = bf16[6,256,24,64]{1,3,2,0:T(8,128)(2,1)} copy(bf16[6,256,24,64]{3,2,1,0:T(8,128)(2,1)} %reshape.634) | data formatting | bytes 9437184
  46.2 8.0 %fusion.94 = f32[6,24,64,128]{3,2,1,0:T(8,128)} fusion(bf16[6,256,24,64]{1,3,2,0:T(8,128)(2,1)} %copy.231, f32[6,256,128]{1,2,0:T(8,128)S(1)} %copy.228, f32[6,24,256]{2,1,0:T(8,128)S(1)} %select_multiply_fusion.3), kind=kOutput, calls=%fused_computation.172 | convolution fusion | flops 613416960 | bytes 10371072 | tf_op jit(solution)/shard_map/jvp(cjhp,chjn->chpn)/dot_general | solution.py:31
  54.2 8.2 %while.108 = (s32[]{:T(128)}, f32[24,64,128]{2,1,0:T(8,128)S(1)}, f32[6,24]{1,0:T(8,128)S(1)}, f32[6,24,64,128]{3,2,1,0:T(8,128)}, s32[]{:T(128)}, /*index=5*/s32[]{:T(128)}) while((s32[]{:T(128)}, f32[24,64,128]{2,1,0:T(8,128)S(1)}, f32[6,24]{1,0:T(8,128)S(1)}, f32[6,24,64,128]{3,2,1,0:T(8,128)}, s32[]{:T(128)}, ...), condition=%wide.region_7.8_spmd.clone, body=%wide.region_6.7_spmd.clone.sunk | while | flops 589827 | bytes 2359671 | solution.py:42
  62.4 83.2 %all-gather.3.cloned.1.call-done = f32[64,12,64,128]{3,2,1,0:T(8,128)} async-done(((f32[1,12,64,128]{3,2,1,0:T(8,128)}), f32[64,12,64,128]{3,2,1,0:T(8,128)}) %all-gather.3.cloned.1.call-update) | async-done | bytes 25165840 | tf_op jit(solution)/shard_map/all_gather | solution.py:104
  157.7 17.0 %while.105 = (s32[]{:T(128)}, f32[24,64,128]{2,1,0:T(8,128)S(1)}, f32[6,24,64,128]{3,2,1,0:T(8,128)}, f32[6,24,1,1]{1,3,2,0:T(1,128)}, f32[6,24]{1,0:T(8,128)S(1)}, /*index=5*/f32[6,24,64,128]{3,2,1,0:T(8,128)}, s32[]{:T(128)}) while((s32[]{:T(128)}, f32[24,64,128]{2,1,0:T(8,128)S(1)}, f32[6,24,64,128]{3,2,1,0:T(8,128)}, ...), condition=%wide.region_9.10_spmd, body=%wide.region_8.9_spmd.sunk | while | flops 393218 | bytes 3934165 | solution.py:42
  181.7 195.7 %while.109 = (s32[]{:T(128)}, f32[24]{0:T(128)}, f32[24]{0:T(128)}, f32[24]{0:T(128)}, bf16[6,256,24,64]{1,3,2,0:T(8,128)(2,1)}, /*index=5*/bf16[6,256,256]{1,2,...) while((s32[]{:T(128)}, f32[24]{0:T(128)}, f32[24]{0:T(128)}, ...), condition=%wide.region_31.32_spmd.clone, body=%wide.region_16.31_spmd.clone.sunk | while | flops 2306163200 | bytes 22004424 | solution.py:79
  193.2 6.2 %fusion.183 = (f32[24,256]{1,0:T(8,128)S(1)}, f32[24,256]{1,0:T(8,128)S(1)}, f32[24,256]{1,0:T(8,128)}, bf16[256,256]{1,0:T(8,128)(2,1)S(1)}) fusion(f32[24,256]{1,0:T(8,128)S(1)} %copy_bitcast_fusion.13, f32[24,256]{1,0:T(8,128)} %get-tuple-element.1559, f32[256,256]{1,0:T(8,128)S(1)} %fusion.181, pred[256,256]{1,0:T(8,128)(4,1)S(1)} %fusion.182, ...), kind=kOutput, calls=%fused_computation.73.clone.1 | convolution fusion | flops 224835584 | bytes 2154496 | tf_op jit(solution)/shard_map/transpose(jvp())/while/body/eval_jaxpr/checkpoint/hij,jhp->ihp/dot_general | solution.py:55
  205.2 3.9 fusion.189
  225.8 6.2 %fusion.183 = (f32[24,256]{1,0:T(8,128)S(1)}, f32[24,256]{1,0:T(8,128)S(1)}, f32[24,256]{1,0:T(8,128)}, bf16[256,256]{1,0:T(8,128)(2,1)S(1)}) fusion(f32[24,256]{1,0:T(8,128)S(1)} %copy_bitcast_fusion.13, f32[24,256]{1,0:T(8,128)} %get-tuple-element.1559, f32[256,256]{1,0:T(8,128)S(1)} %fusion.181, pred[256,256]{1,0:T(8,128)(4,1)S(1)} %fusion.182, ...), kind=kOutput, calls=%fused_computation.73.clone.1 | convolution fusion | flops 224835584 | bytes 2154496 | tf_op jit(solution)/shard_map/transpose(jvp())/while/body/eval_jaxpr/checkpoint/hij,jhp->ihp/dot_general | solution.py:55
  237.8 3.9 fusion.189
  258.4 6.2 %fusion.183 = (f32[24,256]{1,0:T(8,128)S(1)}, f32[24,256]{1,0:T(8,128)S(1)}, f32[24,256]{1,0:T(8,128)}, bf16[256,256]{1,0:T(8,128)(2,1)S(1)}) fusion(f32[24,256]{1,0:T(8,128)S(1)} %copy_bitcast_fusion.13, f32[24,256]{1,0:T(8,128)} %get-tuple-element.1559, f32[256,256]{1,0:T(8,128)S(1)} %fusion.181, pred[256,256]{1,0:T(8,128)(4,1)S(1)} %fusion.182, ...), kind=kOutput, calls=%fused_computation.73.clone.1 | convolution fusion | flops 224835584 | bytes 2154496 | tf_op jit(solution)/shard_map/transpose(jvp())/while/body/eval_jaxpr/checkpoint/hij,jhp->ihp/dot_general | solution.py:55
  270.4 3.9 fusion.189
  291.0 6.2 %fusion.183 = (f32[24,256]{1,0:T(8,128)S(1)}, f32[24,256]{1,0:T(8,128)S(1)}, f32[24,256]{1,0:T(8,128)}, bf16[256,256]{1,0:T(8,128)(2,1)S(1)}) fusion(f32[24,256]{1,0:T(8,128)S(1)} %copy_bitcast_fusion.13, f32[24,256]{1,0:T(8,128)} %get-tuple-element.1559, f32[256,256]{1,0:T(8,128)S(1)} %fusion.181, pred[256,256]{1,0:T(8,128)(4,1)S(1)} %fusion.182, ...), kind=kOutput, calls=%fused_computation.73.clone.1 | convolution fusion | flops 224835584 | bytes 2154496 | tf_op jit(solution)/shard_map/transpose(jvp())/while/body/eval_jaxpr/checkpoint/hij,jhp->ihp/dot_general | solution.py:55
  303.0 3.9 fusion.189
  323.7 6.2 %fusion.183 = (f32[24,256]{1,0:T(8,128)S(1)}, f32[24,256]{1,0:T(8,128)S(1)}, f32[24,256]{1,0:T(8,128)}, bf16[256,256]{1,0:T(8,128)(2,1)S(1)}) fusion(f32[24,256]{1,0:T(8,128)S(1)} %copy_bitcast_fusion.13, f32[24,256]{1,0:T(8,128)} %get-tuple-element.1559, f32[256,256]{1,0:T(8,128)S(1)} %fusion.181, pred[256,256]{1,0:T(8,128)(4,1)S(1)} %fusion.182, ...), kind=kOutput, calls=%fused_computation.73.clone.1 | convolution fusion | flops 224835584 | bytes 2154496 | tf_op jit(solution)/shard_map/transpose(jvp())/while/body/eval_jaxpr/checkpoint/hij,jhp->ihp/dot_general | solution.py:55
  335.7 3.9 fusion.189
  356.3 6.2 %fusion.183 = (f32[24,256]{1,0:T(8,128)S(1)}, f32[24,256]{1,0:T(8,128)S(1)}, f32[24,256]{1,0:T(8,128)}, bf16[256,256]{1,0:T(8,128)(2,1)S(1)}) fusion(f32[24,256]{1,0:T(8,128)S(1)} %copy_bitcast_fusion.13, f32[24,256]{1,0:T(8,128)} %get-tuple-element.1559, f32[256,256]{1,0:T(8,128)S(1)} %fusion.181, pred[256,256]{1,0:T(8,128)(4,1)S(1)} %fusion.182, ...), kind=kOutput, calls=%fused_computation.73.clone.1 | convolution fusion | flops 224835584 | bytes 2154496 | tf_op jit(solution)/shard_map/transpose(jvp())/while/body/eval_jaxpr/checkpoint/hij,jhp->ihp/dot_general | solution.py:55
  368.3 3.9 fusion.189
  377.5 11.6 %while.110 = (s32[]{:T(128)}, f32[24,64,128]{2,1,0:T(8,128)S(1)}, f32[6,24,64,128]{3,2,1,0:T(8,128)}, f32[6,24,1,1]{1,3,2,0:T(1,128)}, s32[]{:T(128)}, /*index=5*/s32[]{:T(128)}, s32[]{:T(128)}) while((s32[]{:T(128)}, f32[24,64,128]{2,1,0:T(8,128)S(1)}, f32[6,24,64,128]{3,2,1,0:T(8,128)}, f32[6,24,1,1]{1,3,2,0:T(1,128)}, ...), condition=%wide.region_33.34_spmd.clone, body=%wide.region_32.33_spmd.clone.sunk | while | flops 589828 | bytes 2359691 | solution.py:42
  394.3 15.2 %while.106 = (s32[]{:T(128)}, f32[24,64,128]{2,1,0:T(8,128)S(1)}, bf16[6,24,64,128]{3,2,1,0:T(8,128)(2,1)S(1)}, f32[6,24]{1,0:T(8,128)S(1)}, f32[6,24,64,128]{3,...) while((s32[]{:T(128)}, f32[24,64,128]{2,1,0:T(8,128)S(1)}, ...), condition=%wide.region_36.37_spmd, body=%wide.region_34.36_spmd.sunk | while | flops 786411 | bytes 4719297 | solution.py:42
  410.9 7.1 %fusion.87 = (f32[6,24,256]{2,1,0:T(8,128)S(1)}, bf16[6,256,128]{1,2,0:T(8,128)(2,1)S(1)}) fusion(f32[6,256,128]{1,2,0:T(8,128)} %copy-done.6, f32[6,24,256]{2,1,0:T(8,128)S(1)} %copy-done.16, bf16[6,24,64,128]{3,2,1,0:T(8,128)(2,1)} %copy-done.4, bf16[6,256,24,64]{1,3,2,0:T(8,128)(2,1)} %get-tuple-element.1777), kind=kOutput, calls=%fused_computation.162 | convolution fusion | flops 627339264 | bytes 8552448 | tf_op jit(solution)/shard_map/transpose(jvp(cjhp,chjn->chpn))/dot_general | solution.py:31
  418.8 14.9 %reduce-window.130 = f32[6,24,2,128]{3,1,2,0:T(8,128)S(1)} reduce-window(f32[6,24,2,128]{3,1,2,0:T(8,128)S(1)} %copy_bitcast_fusion.5, f32[]{:T(128)} %constant.289.clone.1), window={size=1x1x1x128 pad=0_0x0_0x0_0x0_127}, to_apply=%region_40.41 | reduce-window | flops 4681728 | bytes 294916 | tf_op jit(solution)/shard_map/reduce-window.14
  436.3 6.9 %bitcast_add_fusion.6 = bf16[6,256,24,64]{1,3,2,0:T(8,128)(2,1)} fusion(bf16[6,256,24,64]{1,3,2,0:T(8,128)(2,1)} %get-tuple-element.766, bf16[6,24,64,128]{3,2,1,0:T(8,128)(2,1)} %copy-done.4, f32[6,256,128]{1,2,0:T(8,128)S(1)} %copy-done.7, f32[6,24,256]{2,1,0:T(8,128)S(1)} %copy-done.16), kind=kOutput, calls=%fused_computation.171 | convolution fusion | flops 615776256 | bytes 12730368 | tf_op jit(solution)/shard_map/transpose(jvp(cjhp,chjn->chpn))/dot_general | solution.py:31
  443.2 10.4 %copy.250 = bf16[6,256,24,64]{3,2,1,0:T(8,128)(2,1)} copy(bf16[6,256,24,64]{1,3,2,0:T(8,128)(2,1)} %bitcast_add_fusion.6) | data formatting | bytes 9437184
  453.6 13.1 %reshape.633 = bf16[1,1536,1536]{2,1,0:T(8,128)(2,1)} reshape(bf16[6,256,24,64]{3,2,1,0:T(8,128)(2,1)} %copy.250) | data formatting | bytes 9437184
  467.4 62.6 %while.107 = (s32[]{:T(128)}, bf16[6,256,1536]{2,1,0:T(8,128)(2,1)}, bf16[6,256,24,64]{1,3,2,0:T(8,128)(2,1)}, bf16[6,256,256]{2,1,0:T(8,128)(2,1)}, s32[6,256]{...) while((s32[]{:T(128)}, bf16[6,256,1536]{2,1,0:T(8,128)(2,1)}, ...), condition=%wide.region_15.16_spmd.clone, body=%wide.region_10.15_spmd.clone.sunk | while | flops 833433920 | bytes 10981461 | solution.py:79
  473.3 3.5 fusion.167
  494.0 3.6 fusion.167
  514.8 3.6 fusion.167
  525.2 3.5 fusion.167
  530.0 64.5 %all-reduce.5 = (f32[24]{0:T(128)}, f32[24]{0:T(128)}, f32[24]{0:T(128)}) all-reduce(f32[24]{0:T(128)S(1)} %get-tuple-element.1226, f32[24]{0:T(128)S(1)} %add.228, f32[24]{0:T(128)S(1)} %copy-done.26), channel_id=1, replica_groups=mesh['stream'=64,'seq'=2] {'stream','seq'}, use_global_device_ids=true, to_apply=%region_43.44 | all-reduce | flops 72 | bytes 576 | tf_op jit(solution)/shard_map/psum | solution.py:154
  (709 shorter events, 276.4 us)
Async XLA Ops:
  7.2 138.5 %all-gather.3.cloned.1.call-start = ((), (), s32[]{:S(2)}) async-start(), calls=%async_computation | async-start | bytes 25559040 | tf_op jit(solution)/shard_map/all_gather | solution.py:104
  14.3 19.8 %copy-start.32 = (f32[24]{0:T(128)}, f32[24]{0:T(128)S(1)}, u32[]{:S(2)}) copy-start(f32[24]{0:T(128)S(1)} %exp.90) | copy-start | bytes 292
  16.1 29.9 %copy-start.1 = (f32[6,24,256]{2,1,0:T(8,128)}, f32[6,24,256]{2,1,0:T(8,128)S(1)}, u32[]{:S(2)}) copy-start(f32[6,24,256]{2,1,0:T(8,128)S(1)} %get-tuple-element.1738) | copy-start | bytes 442372
  19.9 26.1 %copy-start.11 = (f32[6,24,2]{1,2,0:T(2,128)}, f32[6,24,2]{1,2,0:T(2,128)S(1)}, u32[]{:S(2)}) copy-start(f32[6,24,2]{1,2,0:T(2,128)S(1)} %slice.164) | copy-start | bytes 3460
  21.2 25.0 %copy-start.6 = (f32[6,256,128]{1,2,0:T(8,128)}, f32[6,256,128]{1,2,0:T(8,128)S(1)}, u32[]{:S(2)}) copy-start(f32[6,256,128]{1,2,0:T(8,128)S(1)} %copy.228) | copy-start | bytes 2359300
  34.1 11.9 %copy-start.10 = (f32[24]{0:T(128)S(1)}, f32[24]{0:T(128)}, u32[]{:S(2)}) copy-start(f32[24]{0:T(128)} %param.26) | copy-start | bytes 292
  45.3 8.9 %copy-start.13 = (f32[6,24]{1,0:T(8,128)}, f32[6,24]{1,0:T(8,128)S(1)}, u32[]{:S(2)}) copy-start(f32[6,24]{1,0:T(8,128)S(1)} %slice_reduce_fusion.7) | copy-start | bytes 1732
  46.0 8.2 %copy-start.19 = (pred[6,256]{1,0:T(8,128)(4,1)}, pred[6,256]{1,0:T(8,128)(4,1)S(1)}, u32[]{:S(2)}) copy-start(pred[6,256]{1,0:T(8,128)(4,1)S(1)} %broadcast_compare_fusion.2) | copy-start | bytes 4612
  150.3 4.4 collective-permute-start
  205.2 8.0 %copy-start.21 = (f32[24]{0:T(128)S(1)}, f32[24]{0:T(128)}, u32[]{:S(2)}) copy-start(f32[24]{0:T(128)} %get-tuple-element.1641) | copy-start | bytes 292 | tf_op jit(solution)/shard_map/transpose(jvp())/while
  205.2 8.0 %copy-start.27 = (f32[24]{0:T(128)S(1)}, f32[24]{0:T(128)}, u32[]{:S(2)}) copy-start(f32[24]{0:T(128)} %get-tuple-element.1642) | copy-start | bytes 292 | tf_op jit(solution)/shard_map/transpose(jvp())/while
  237.8 8.0 %copy-start.21 = (f32[24]{0:T(128)S(1)}, f32[24]{0:T(128)}, u32[]{:S(2)}) copy-start(f32[24]{0:T(128)} %get-tuple-element.1641) | copy-start | bytes 292 | tf_op jit(solution)/shard_map/transpose(jvp())/while
  237.8 8.0 %copy-start.27 = (f32[24]{0:T(128)S(1)}, f32[24]{0:T(128)}, u32[]{:S(2)}) copy-start(f32[24]{0:T(128)} %get-tuple-element.1642) | copy-start | bytes 292 | tf_op jit(solution)/shard_map/transpose(jvp())/while
  270.4 8.0 %copy-start.21 = (f32[24]{0:T(128)S(1)}, f32[24]{0:T(128)}, u32[]{:S(2)}) copy-start(f32[24]{0:T(128)} %get-tuple-element.1641) | copy-start | bytes 292 | tf_op jit(solution)/shard_map/transpose(jvp())/while
  270.4 8.0 %copy-start.27 = (f32[24]{0:T(128)S(1)}, f32[24]{0:T(128)}, u32[]{:S(2)}) copy-start(f32[24]{0:T(128)} %get-tuple-element.1642) | copy-start | bytes 292 | tf_op jit(solution)/shard_map/transpose(jvp())/while
  303.0 8.0 %copy-start.27 = (f32[24]{0:T(128)S(1)}, f32[24]{0:T(128)}, u32[]{:S(2)}) copy-start(f32[24]{0:T(128)} %get-tuple-element.1642) | copy-start | bytes 292 | tf_op jit(solution)/shard_map/transpose(jvp())/while
  335.7 8.0 %copy-start.27 = (f32[24]{0:T(128)S(1)}, f32[24]{0:T(128)}, u32[]{:S(2)}) copy-start(f32[24]{0:T(128)} %get-tuple-element.1642) | copy-start | bytes 292 | tf_op jit(solution)/shard_map/transpose(jvp())/while
  368.3 8.0 %copy-start.21 = (f32[24]{0:T(128)S(1)}, f32[24]{0:T(128)}, u32[]{:S(2)}) copy-start(f32[24]{0:T(128)} %get-tuple-element.1641) | copy-start | bytes 292 | tf_op jit(solution)/shard_map/transpose(jvp())/while
  368.3 8.0 %copy-start.27 = (f32[24]{0:T(128)S(1)}, f32[24]{0:T(128)}, u32[]{:S(2)}) copy-start(f32[24]{0:T(128)} %get-tuple-element.1642) | copy-start | bytes 292 | tf_op jit(solution)/shard_map/transpose(jvp())/while
  377.5 11.6 %copy-start.34 = (f32[24]{0:T(128)S(1)}, f32[24]{0:T(128)}, u32[]{:S(2)}) copy-start(f32[24]{0:T(128)} %broadcast_multiply_fusion) | copy-start | bytes 292
  390.1 4.1 collective-permute-start.1
  394.2 15.2 %copy-start.14 = (f32[6,24]{1,0:T(8,128)S(1)}, f32[6,24]{1,0:T(8,128)}, u32[]{:S(2)}) copy-start(f32[6,24]{1,0:T(8,128)} %copy-done.13) | copy-start | bytes 1732
  394.2 15.2 %copy-start.31 = (pred[6]{0:T(512)(128)(4,1)S(1)}, pred[6]{0:T(512)(128)(4,1)}, u32[]{:S(2)}) copy-start(pred[6]{0:T(512)(128)(4,1)} %copy-done.30) | copy-start | bytes 22
  394.2 16.6 %copy-start.16 = (f32[6,24,256]{2,1,0:T(8,128)S(1)}, f32[6,24,256]{2,1,0:T(8,128)}, u32[]{:S(2)}) copy-start(f32[6,24,256]{2,1,0:T(8,128)} %copy-done.15) | copy-start | bytes 442372
  410.9 23.0 %copy-start.33 = (f32[24]{0:T(128)S(1)}, f32[24]{0:T(128)}, u32[]{:S(2)}) copy-start(f32[24]{0:T(128)} %copy-done.32) | copy-start | bytes 292
  410.9 23.4 %copy-start.9 = (f32[6,24,256]{2,1,0:T(8,128)S(1)}, f32[6,24,256]{2,1,0:T(8,128)}, u32[]{:S(2)}) copy-start(f32[6,24,256]{2,1,0:T(8,128)} %get-tuple-element.772) | copy-start | bytes 442372
  410.9 24.2 %copy-start.3 = (bf16[6,256,256]{1,2,0:T(8,128)(2,1)S(1)}, bf16[6,256,256]{1,2,0:T(8,128)(2,1)}, u32[]{:S(2)}) copy-start(bf16[6,256,256]{1,2,0:T(8,128)(2,1)} %get-tuple-element.771) | copy-start | bytes 2359300
  418.0 18.4 %copy-start.7 = (f32[6,256,128]{1,2,0:T(8,128)S(1)}, f32[6,256,128]{1,2,0:T(8,128)}, u32[]{:S(2)}) copy-start(f32[6,256,128]{1,2,0:T(8,128)} %copy-done.6) | copy-start | bytes 2359300
  453.6 13.1 %copy-start.23 = (f32[24]{0:T(128)S(1)}, f32[24]{0:T(128)}, u32[]{:S(2)}) copy-start(f32[24]{0:T(128)} %get-tuple-element.774) | copy-start | bytes 292
  453.6 13.7 %copy-start.35 = (f32[24]{0:T(128)S(1)}, f32[24]{0:T(128)}, u32[]{:S(2)}) copy-start(f32[24]{0:T(128)} %get-tuple-element.1787) | copy-start | bytes 292
  467.4 62.7 %copy-start.29 = (f32[24]{0:T(128)S(1)}, f32[24]{0:T(128)}, u32[]{:S(2)}) copy-start(f32[24]{0:T(128)} %get-tuple-element.775) | copy-start | bytes 292
  467.4 62.7 %copy-start.26 = (f32[24]{0:T(128)S(1)}, f32[24]{0:T(128)}, u32[]{:S(2)}) copy-start(f32[24]{0:T(128)} %get-tuple-element.776) | copy-start | bytes 292
  (62 other events, 269.2 us)
Sparse Core Ops, SparseCore 0:
  10.8 134.8 all-gather.2
where the time goes:
time: 607 us; the launch traced here: 601 us
  local copies, waits for them, and re-layouts  158 us (26%)
  matrix products  151 us (25%)
  other arithmetic  115 us (19%)
  waiting for transfers between devices  86.9 us (14%)
  blocking collectives  67.2 us (11%)
  between operations  16.4 us (3%)
    all_gather x1, waiting for transfers between devices, shards(): gathered = lax.all_gather(old_states, 'stream', axis=0, tiled=True)  83.2 us
    dot_general x18, matrix products, one_group(): jnp.einsum('hij,jhp->ihp', mixing, inputs_q, preferred_element_type=jnp.f...  81.8 us
    psum x1, blocking collectives, shards(): lax.psum((rates_first + rates_second, bias_first + bias_second, skip_tota...  64.5 us
    another operation x80, other arithmetic  52.5 us
    dot_general x24, matrix products, one_group(): jnp.einsum('in,hpn->ihp', c_part.astype(jnp.float32), starts_q, precision...  43.1 us
    unnamed x56, local copies, waits for them, and re-layouts  35.7 us
    squeeze x30, local copies, waits for them, and re-layouts, outputs(): lax.scan(per_group, 0, (inputs_c, maps_c, logits_c, flags_c, starts_c))  22.8 us
    dot_general x3, matrix products, group_states(): jnp.einsum('cjhp,chjn->chpn', inputs_c, b_weighted, preferred_element_typ...  21.9 us
  transfers between devices with their start and end apart: 3, of which 3 were waited for; matrix products, arithmetic and copies ran while one was open for 9% of the time, Pallas kernels for 0%

commit v1 on v0

--- a/solution.py
+++ b/solution.py
@@ -101,7 +101,11 @@
     stream_index = lax.axis_index("stream")
     position = seq_index * length + lax.iota(jnp.int32, length)
     reset_flags = jnp.any(doc_starts[0][:, None] == position[None, :], axis=0).astype(jnp.int32)
-    gathered = lax.all_gather(old_states, "stream", axis=0, tiled=True)
+    supply_all_row_for = lambda raw: jnp.concatenate(
+        lax.all_to_all(jnp.stack([raw for _ in range(lax.axis_size("stream"))], 0), "stream", 0, 0),
+        0,
+    )
+    gathered = supply_all_row_for(old_states)
     own_block = lax.dynamic_index_in_dim(gathered, old_owner[stream_index], 0, keepdims=False)
     start_state = lax.all_gather(own_block, "seq", axis=0, tiled=True)
     inputs_c = head_inputs[0].reshape(groups, GROUP, head_count, head_dim)

time: 607 us -> 935 us (1.54)
  waiting for transfers between devices: 86.9 us -> 398 us
  between operations: 16.4 us -> 3.1 us
  starting transfers between devices: 3.8 us -> 16.1 us
  local copies, waits for them, and re-layouts: 158 us -> 169 us
    all_to_all x0 -> x1, waiting for transfers between devices: none -> 395 us  [shards(): lax.all_to_all(jnp.stack([raw for _ in range(lax.axis_size('stream'))], 0...]
    all_gather x1 -> x0, waiting for transfers between devices: 83.2 us -> none  [shards(): gathered = lax.all_gather(old_states, 'stream', axis=0, tiled=True)]
    another operation x83 -> x84, local copies, waits for them, and re-layouts: 11 us -> 23.6 us  [the longest x1 12.5 us: shards(): jnp.stack([raw for _ in range(lax.axis_size('stream'))], 0)]
    all_to_all x0 -> x1, starting transfers between devices: none -> 12.3 us  [shards(): lax.all_to_all(jnp.stack([raw for _ in range(lax.axis_size('stream'))], 0...]
    unnamed x56 -> x64, local copies, waits for them, and re-layouts: 35.7 us -> 35.6 us
  transfers between devices with their start and end apart: 3 -> 3, of which waited for: 3 -> 3; matrix products, arithmetic and copies ran while one was open for 9% -> 5% of each run, Pallas kernels for 0% -> 0%
where the time goes in v1:
time: 935 us; the launch traced here: 929 us
  waiting for transfers between devices  398 us (43%)
  local copies, waits for them, and re-layouts  169 us (18%)
  matrix products  151 us (16%)
  other arithmetic  113 us (12%)
  blocking collectives  76.2 us (8%)
  starting transfers between devices  16.1 us (2%)
    all_to_all x1, waiting for transfers between devices, shards(): lax.all_to_all(jnp.stack([raw for _ in range(lax.axis_size('stream'))], 0...  395 us
    dot_general x18, matrix products, one_group(): jnp.einsum('hij,jhp->ihp', mixing, inputs_q, preferred_element_type=jnp.f...  81.8 us
    psum x1, blocking collectives, shards(): lax.psum((rates_first + rates_second, bias_first + bias_second, skip_tota...  72.1 us
    another operation x80, other arithmetic  52.5 us
    dot_general x24, matrix products, one_group(): jnp.einsum('in,hpn->ihp', c_part.astype(jnp.float32), starts_q, precision...  43.1 us
    unnamed x64, local copies, waits for them, and re-layouts  35.6 us
    squeeze x30, local copies, waits for them, and re-layouts, outputs(): lax.scan(per_group, 0, (inputs_c, maps_c, logits_c, flags_c, starts_c))  22.8 us
    dot_general x3, matrix products, group_states(): jnp.einsum('cjhp,chjn->chpn', inputs_c, b_weighted, preferred_element_typ...  21.9 us
  transfers between devices with their start and end apart: 3, of which 3 were waited for; matrix products, arithmetic and copies ran while one was open for 5% of the time, Pallas kernels for 0%

profile of v1, /device:TPU:1, one launch (start us, length us, event | category | flops | bytes accessed | tf_op | source)
XLA Modules:
  0.0 929.1 jit_solution(4669470102375340444)
XLA Ops:
  0.6 12.5 %stack.2 = f32[64,1,12,64,128]{4,3,1,2,0:T(8,128)} broadcast(f32[12,64,128]{2,1,0:T(8,128)} %bitcast.404), dimensions={2,3,4} | broadcast | bytes 25559040 | tf_op jit(solution)/shard_map/stack | solution.py:105
  13.2 12.3 %all-to-all-start = ((f32[64,1,12,64,128]{4,3,1,2,0:T(8,128)}), f32[64,1,12,64,128]{4,3,1,2,0:T(8,128)}, u32[]{:S(2)}, u32[]{:S(2)}) async-start(f32[64,1,12,64,128]{4,3,1,2,0:T(8,128)} %stack.2), calls=%async_computation | async-start | bytes 50331648 | tf_op jit(solution)/shard_map/all_to_all | solution.py:105
  35.0 12.8 %reshape.640 = bf16[6,256,24,64]{3,2,1,0:T(8,128)(2,1)} reshape(bf16[1,1536,1536]{2,1,0:T(8,128)(2,1)} %param.22) | data formatting | bytes 9437184 | tf_op jit(solution)/shard_map/reshape;squeeze | solution.py:111
  47.8 10.3 %copy.263 = bf16[6,256,24,64]{1,3,2,0:T(8,128)(2,1)} copy(bf16[6,256,24,64]{3,2,1,0:T(8,128)(2,1)} %reshape.640) | data formatting | bytes 9437184
  59.9 8.0 fusion.94
  67.8 7.9 while.108
  75.7 395.5 %all-to-all-done = f32[64,1,12,64,128]{4,3,1,2,0:T(8,128)} async-done(((f32[64,1,12,64,128]{4,3,1,2,0:T(8,128)}), f32[64,1,12,64,128]{4,3,1,2,0:T(8,128)}, u32[]{:S(2)}, u32[]{:S(2)}) %all-to-all-start) | async-done | bytes 25165856 | tf_op jit(solution)/shard_map/all_to_all | solution.py:105
  472.2 4.1 all-gather
  484.6 17.0 %while.105 = (s32[]{:T(128)}, f32[24,64,128]{2,1,0:T(8,128)S(1)}, f32[6,24,64,128]{3,2,1,0:T(8,128)}, f32[6,24,1,1]{1,3,2,0:T(1,128)}, f32[6,24]{1,0:T(8,128)S(1)}, /*index=5*/f32[6,24,64,128]{3,2,1,0:T(8,128)}, s32[]{:T(128)}) while((s32[]{:T(128)}, f32[24,64,128]{2,1,0:T(8,128)S(1)}, f32[6,24,64,128]{3,2,1,0:T(8,128)}, ...), condition=%wide.region_9.10_spmd, body=%wide.region_8.9_spmd.sunk | while | flops 393218 | bytes 3934165 | solution.py:42
  508.7 195.7 %while.109 = (s32[]{:T(128)}, f32[24]{0:T(128)}, f32[24]{0:T(128)}, f32[24]{0:T(128)}, bf16[6,256,24,64]{1,3,2,0:T(8,128)(2,1)}, /*index=5*/bf16[6,256,256]{1,2,...) while((s32[]{:T(128)}, f32[24]{0:T(128)}, f32[24]{0:T(128)}, ...), condition=%wide.region_31.32_spmd.clone, body=%wide.region_16.31_spmd.clone.sunk | while | flops 2306163200 | bytes 22004424 | solution.py:79
  520.2 6.2 fusion.183
  532.1 3.9 fusion.189
  552.8 6.2 fusion.183
  564.8 3.9 fusion.189
  585.4 6.2 fusion.183
  597.4 3.9 fusion.189
  618.0 6.2 fusion.183
  630.0 3.9 fusion.189
  650.6 6.2 fusion.183
  662.7 3.9 fusion.189
  683.3 6.2 fusion.183
  695.3 3.9 fusion.189
  704.5 11.6 %while.110 = (s32[]{:T(128)}, f32[24,64,128]{2,1,0:T(8,128)S(1)}, f32[6,24,64,128]{3,2,1,0:T(8,128)}, f32[6,24,1,1]{1,3,2,0:T(1,128)}, s32[]{:T(128)}, /*index=5*/s32[]{:T(128)}, s32[]{:T(128)}) while((s32[]{:T(128)}, f32[24,64,128]{2,1,0:T(8,128)S(1)}, f32[6,24,64,128]{3,2,1,0:T(8,128)}, f32[6,24,1,1]{1,3,2,0:T(1,128)}, ...), condition=%wide.region_33.34_spmd.clone, body=%wide.region_32.33_spmd.clone.sunk | while | flops 589828 | bytes 2359691 | solution.py:42
  721.2 15.2 %while.106 = (s32[]{:T(128)}, f32[24,64,128]{2,1,0:T(8,128)S(1)}, bf16[6,24,64,128]{3,2,1,0:T(8,128)(2,1)S(1)}, f32[6,24]{1,0:T(8,128)S(1)}, f32[6,24,64,128]{3,...) while((s32[]{:T(128)}, f32[24,64,128]{2,1,0:T(8,128)S(1)}, ...), condition=%wide.region_36.37_spmd, body=%wide.region_34.36_spmd.sunk | while | flops 786411 | bytes 4719297 | solution.py:42
  737.9 7.1 fusion.87
  745.7 14.9 %reduce-window.130 = f32[6,24,2,128]{3,1,2,0:T(8,128)S(1)} reduce-window(f32[6,24,2,128]{3,1,2,0:T(8,128)S(1)} %copy_bitcast_fusion.5, f32[]{:T(128)} %constant.290.clone.1), window={size=1x1x1x128 pad=0_0x0_0x0_0x0_127}, to_apply=%region_40.41 | reduce-window | flops 4681728 | bytes 294916 | tf_op jit(solution)/shard_map/reduce-window.14
  763.3 6.9 bitcast_add_fusion.6
  770.2 10.4 %copy.282 = bf16[6,256,24,64]{3,2,1,0:T(8,128)(2,1)} copy(bf16[6,256,24,64]{1,3,2,0:T(8,128)(2,1)} %bitcast_add_fusion.6) | data formatting | bytes 9437184
  780.6 13.1 %reshape.639 = bf16[1,1536,1536]{2,1,0:T(8,128)(2,1)} reshape(bf16[6,256,24,64]{3,2,1,0:T(8,128)(2,1)} %copy.282) | data formatting | bytes 9437184
  794.3 62.6 %while.107 = (s32[]{:T(128)}, bf16[6,256,1536]{2,1,0:T(8,128)(2,1)}, bf16[6,256,24,64]{1,3,2,0:T(8,128)(2,1)}, bf16[6,256,256]{2,1,0:T(8,128)(2,1)}, s32[6,256]{...) while((s32[]{:T(128)}, bf16[6,256,1536]{2,1,0:T(8,128)(2,1)}, ...), condition=%wide.region_15.16_spmd.clone, body=%wide.region_10.15_spmd.clone.sunk | while | flops 833433920 | bytes 10981461 | solution.py:79
  852.1 3.6 fusion.167
  856.9 72.1 %all-reduce.5 = (f32[24]{0:T(128)}, f32[24]{0:T(128)}, f32[24]{0:T(128)}) all-reduce(f32[24]{0:T(128)S(1)} %get-tuple-element.1260, f32[24]{0:T(128)S(1)} %add.228, f32[24]{0:T(128)S(1)} %copy-done.28), channel_id=1, replica_groups=mesh['stream'=64,'seq'=2] {'stream','seq'}, use_global_device_ids=true, to_apply=%region_43.44 | all-reduce | flops 72 | bytes 576 | tf_op jit(solution)/shard_map/psum | solution.py:158
  (717 shorter events, 279.3 us)
Async XLA Ops:
  13.2 12.4 %copy-start.38 = (s32[64]{0:T(128)S(1)}, s32[64]{0:T(128)}, u32[]{:S(2)}) copy-start(s32[64]{0:T(128)} %param.29) | copy-start | bytes 772
  13.2 14.3 %copy-start.37 = (s32[1,2]{1,0:T(1,128)S(1)}, s32[1,2]{1,0:T(1,128)}, u32[]{:S(2)}) copy-start(s32[1,2]{1,0:T(1,128)} %param.30) | copy-start | bytes 28
  13.2 17.5 %copy-start.16 = (f32[1,24,1536]{2,1,0:T(8,128)S(1)}, f32[1,24,1536]{2,1,0:T(8,128)}, u32[]{:S(2)}) copy-start(f32[1,24,1536]{2,1,0:T(8,128)} %param.24) | copy-start | bytes 442372
  13.2 17.5 %copy-start.11 = (f32[24]{0:T(128)S(1)}, f32[24]{0:T(128)}, u32[]{:S(2)}) copy-start(f32[24]{0:T(128)} %param.26) | copy-start | bytes 292
  13.2 21.5 %copy-start.3 = (bf16[1,1536,256]{2,1,0:T(8,128)(2,1)S(1)}, bf16[1,1536,256]{2,1,0:T(8,128)(2,1)}, u32[]{:S(2)}) copy-start(bf16[1,1536,256]{2,1,0:T(8,128)(2,1)} %param.23) | copy-start | bytes 2359300
  13.2 458.0 %all-to-all-start = ((f32[64,1,12,64,128]{4,3,1,2,0:T(8,128)}), f32[64,1,12,64,128]{4,3,1,2,0:T(8,128)}, u32[]{:S(2)}, u32[]{:S(2)}) async-start(f32[64,1,12,64,128]{4,3,1,2,0:T(8,128)} %stack.2), calls=%async_computation | async-start | bytes 50331648 | tf_op jit(solution)/shard_map/all_to_all | solution.py:105
  30.9 28.7 %copy-start.1 = (f32[6,24,256]{2,1,0:T(8,128)}, f32[6,24,256]{2,1,0:T(8,128)S(1)}, u32[]{:S(2)}) copy-start(f32[6,24,256]{2,1,0:T(8,128)S(1)} %get-tuple-element.1772) | copy-start | bytes 442372
  34.6 25.0 %copy-start.12 = (f32[6,24,2]{1,2,0:T(2,128)}, f32[6,24,2]{1,2,0:T(2,128)S(1)}, u32[]{:S(2)}) copy-start(f32[6,24,2]{1,2,0:T(2,128)S(1)} %slice.164) | copy-start | bytes 3460
  35.0 24.8 %copy-start.7 = (f32[6,256,128]{1,2,0:T(8,128)}, f32[6,256,128]{1,2,0:T(8,128)S(1)}, u32[]{:S(2)}) copy-start(f32[6,256,128]{1,2,0:T(8,128)S(1)} %copy.260) | copy-start | bytes 2359300
  59.1 8.8 copy-start.14
  59.6 8.2 copy-start.21
  477.3 4.4 collective-permute-start
  532.1 8.0 copy-start.29
  564.8 8.0 copy-start.29
  597.4 8.0 copy-start.23
  597.4 8.0 copy-start.29
  630.0 8.0 copy-start.29
  662.6 8.0 copy-start.29
  695.3 8.0 copy-start.29
  704.5 11.6 %copy-start.36 = (f32[24]{0:T(128)S(1)}, f32[24]{0:T(128)}, u32[]{:S(2)}) copy-start(f32[24]{0:T(128)} %broadcast_multiply_fusion) | copy-start | bytes 292
  717.1 4.1 collective-permute-start.1
  721.2 15.2 %copy-start.15 = (f32[6,24]{1,0:T(8,128)S(1)}, f32[6,24]{1,0:T(8,128)}, u32[]{:S(2)}) copy-start(f32[6,24]{1,0:T(8,128)} %copy-done.14) | copy-start | bytes 1732
  721.2 15.2 %copy-start.33 = (pred[6]{0:T(512)(128)(4,1)S(1)}, pred[6]{0:T(512)(128)(4,1)}, u32[]{:S(2)}) copy-start(pred[6]{0:T(512)(128)(4,1)} %copy-done.32) | copy-start | bytes 22
  721.2 16.6 %copy-start.18 = (f32[6,24,256]{2,1,0:T(8,128)S(1)}, f32[6,24,256]{2,1,0:T(8,128)}, u32[]{:S(2)}) copy-start(f32[6,24,256]{2,1,0:T(8,128)} %copy-done.17) | copy-start | bytes 442372
  737.8 23.0 %copy-start.35 = (f32[24]{0:T(128)S(1)}, f32[24]{0:T(128)}, u32[]{:S(2)}) copy-start(f32[24]{0:T(128)} %copy-done.34) | copy-start | bytes 292
  737.8 23.4 %copy-start.10 = (f32[6,24,256]{2,1,0:T(8,128)S(1)}, f32[6,24,256]{2,1,0:T(8,128)}, u32[]{:S(2)}) copy-start(f32[6,24,256]{2,1,0:T(8,128)} %get-tuple-element.772) | copy-start | bytes 442372
  737.9 24.2 %copy-start.4 = (bf16[6,256,256]{1,2,0:T(8,128)(2,1)S(1)}, bf16[6,256,256]{1,2,0:T(8,128)(2,1)}, u32[]{:S(2)}) copy-start(bf16[6,256,256]{1,2,0:T(8,128)(2,1)} %get-tuple-element.771) | copy-start | bytes 2359300
  744.9 18.4 %copy-start.8 = (f32[6,256,128]{1,2,0:T(8,128)S(1)}, f32[6,256,128]{1,2,0:T(8,128)}, u32[]{:S(2)}) copy-start(f32[6,256,128]{1,2,0:T(8,128)} %copy-done.7) | copy-start | bytes 2359300
  780.6 13.1 %copy-start.25 = (f32[24]{0:T(128)S(1)}, f32[24]{0:T(128)}, u32[]{:S(2)}) copy-start(f32[24]{0:T(128)} %get-tuple-element.774) | copy-start | bytes 292
  780.6 13.7 %copy-start.39 = (f32[24]{0:T(128)S(1)}, f32[24]{0:T(128)}, u32[]{:S(2)}) copy-start(f32[24]{0:T(128)} %get-tuple-element.1819) | copy-start | bytes 292
  794.3 62.6 %copy-start.31 = (f32[24]{0:T(128)S(1)}, f32[24]{0:T(128)}, u32[]{:S(2)}) copy-start(f32[24]{0:T(128)} %get-tuple-element.775) | copy-start | bytes 292
  794.3 62.6 %copy-start.28 = (f32[24]{0:T(128)S(1)}, f32[24]{0:T(128)}, u32[]{:S(2)}) copy-start(f32[24]{0:T(128)} %get-tuple-element.776) | copy-start | bytes 292
  (66 other events, 296.8 us)
